TPU v7x, 32 devices: a whole 2x2x4 slice. The times are simulated.
32 devices in a mesh: grp: 4 (over z), sep: 8 (over y, x, core).
Axes of the slice: x: 2, y: 2, z: 4, core: 2. Of those that a mesh axis runs over, the one named last changes fastest.
Arguments:
- tiles: bfloat16 [4, 256, 64, 128], P('grp', 'sep'), may hold values from 0.0099487305 to 0.29882812
- tile_front: int32 [4, 256, 1], P('grp', 'sep'), may hold values from 0 to 7; in each aligned block of 32 rows (0 to 31, 32 to 63, ..., all dimensions but the last counted through in order) at most 8 rows name the same one
- tile_pos: int32 [4, 256], P('grp', 'sep'), may hold values from 0 to 29
- front_slot: int32 [4, 8], P('grp'), may hold values from 0 to 7, as said below
- front_parent: int32 [4, 8], P('grp'), may hold values from 0 to 7, as said below
- pivot: float32 [4, 8, 640], P('grp'), may hold values from 4 to 40
Outputs:
- factor: float32 [4, 8, 640, 512], P('grp', 'sep')
- sep_schur: float32 [8, 128, 128], P('sep')
Inputs may be any that keep to these rules, and one draw needn't show every extreme that they name: `tile_front`: at most 8 of the tiles held by one device belong to one front. `front_slot`: each group's row is a permutation of 0 to 7. (front_parent[g, f] - front_slot[g, f]) modulo 8 is one of 0, 1, 7 and 4; in every group each of these four occurs.
All inputs are finite; a program needn't handle non-finite values.
Results may differ from a plain program's by a relative error of at most 0.0003.
Values may be sent and summed in bfloat16 or wider, within the bound.
A program may use at most 64 MiB of HBM per device.

v0:
```python
import jax
import jax.numpy as jnp
import numpy as np
from jax import lax
from jax.sharding import PartitionSpec as P

POS = 30


def passed_along(shard, axis, by):
    devices = lax.axis_size(axis)
    return lax.ppermute(shard, axis, [(i, (i + by) % devices) for i in range(devices)])


def tile_arrangement(rows, column_indices):
    row_count = 5 * column_indices // rows
    position = np.zeros((row_count, 5), np.int32)
    present = np.zeros((row_count, 5), np.float32)
    number = 0
    for row_block in range(row_count):
        for col_block in range(row_block * rows // column_indices + 1):
            position[row_block, col_block] = number
            present[row_block, col_block] = 1.0
            number += 1
    return (position, present)


def front_factor(summed, pivots, rows, column_indices):
    position, present = tile_arrangement(rows, column_indices)
    order = 5 * column_indices
    elimination_count = 4 * column_indices
    blocks = summed[position] * jnp.asarray(present, jnp.float32)[:, :, None, None]
    full = blocks.transpose(0, 2, 1, 3).reshape(order, order)
    mixed = 0.5 * (full + full.T) * (1.0 - jnp.eye(order, dtype=jnp.float32))
    front_matrix = jnp.diag(pivots + jnp.sum(mixed, 1)) - mixed
    lower_triangle = jnp.linalg.cholesky(front_matrix[:elimination_count, :elimination_count])
    under_diagonal = jax.scipy.linalg.solve_triangular(
        lower_triangle, front_matrix[elimination_count:, :elimination_count].T, lower=True
    ).T
    schur = jnp.dot(under_diagonal, under_diagonal.T, precision=lax.Precision.HIGHEST)
    return (jnp.concatenate([lower_triangle, under_diagonal], 0), schur)


def body(tiles, tile_front, tile_pos, front_slot, front_parent, pivot):
    width = lax.axis_size("sep")
    myself = lax.axis_index("sep")
    held = tiles.shape[1]
    rows = tiles.shape[2]
    column_indices = tiles.shape[3]
    fronts = front_slot.shape[1]
    room = max(2, -(-2 * held // width))
    slots = front_slot[0]
    parents = front_parent[0]
    front_ids = jnp.arange(fronts, dtype=jnp.int32)
    owner_of = jnp.sum(jnp.where(tile_front[0] == front_ids[None, :], slots[None, :], 0), 1)
    target = (owner_of[:, None] == jnp.arange(width, dtype=jnp.int32)[None, :]).astype(jnp.int32)
    rank = jnp.sum(target * (jnp.cumsum(target, 0) - 1), 1)
    place = owner_of * room + rank
    outgoing = jnp.zeros((width * room, rows, column_indices), jnp.bfloat16).at[place].set(tiles[0])
    labels = jnp.full((width * room,), -1, jnp.int32).at[place].set(tile_pos[0])
    arrived, received_position = (
        lax.all_to_all(
            outgoing.reshape(width, room, rows, column_indices),
            "sep",
            split_axis=0,
            concat_axis=0,
            tiled=True,
        ),
        lax.all_to_all(labels.reshape(width, room), "sep", split_axis=0, concat_axis=0, tiled=True),
    )
    arrived = arrived.reshape(width * room, rows, column_indices)
    received_position = received_position.reshape(width * room)
    selector = (received_position[None, :] == jnp.arange(POS, dtype=jnp.int32)[:, None]).astype(
        jnp.bfloat16
    )
    summed = jnp.einsum("ps,sij->pij", selector, arrived, preferred_element_type=jnp.float32)
    mine = slots == myself
    pivots = jnp.sum(jnp.where(mine[:, None], pivot[0], 0.0), 0)
    parent = jnp.sum(jnp.where(mine, parents, 0))
    factor, schur = front_factor(summed, pivots, rows, column_indices)
    distance = (parent - myself) % width
    local_sum = jnp.where(distance == 0, schur, 0.0)[None]
    for offset in (1, -1, width // 2):
        piece = jnp.where(distance == offset % width, schur, 0.0)[None]
        local_sum = local_sum + passed_along(piece, "sep", offset)
    total = lax.psum(local_sum, "grp")
    return (factor[None, None], total)


def solution(mesh):
    placed = (
        P("grp", "sep", None, None),
        P("grp", "sep", None),
        P("grp", "sep"),
        P("grp", None),
        P("grp", None),
        P("grp", None, None),
    )
    return jax.shard_map(
        body,
        mesh=mesh,
        in_specs=placed,
        out_specs=(P("grp", "sep", None, None), P("sep", None, None)),
        check_vma=False,
    )
```

profile of v0, /device:TPU:0, one launch (start us, length us, event | category | flops | bytes accessed | tf_op | source)
XLA Modules:
  0.0 244.2 jit_solution(3018031008141978505)
XLA Ops:
  9.8 5.2 %all-to-all-start = ((s32[8,1,8]{2,1,0:T(1,128)}), s32[8,1,8]{2,1,0:T(1,128)S(1)}, u32[]{:S(2)}, u32[]{:S(2)}) async-start(s32[8,1,8]{2,1,0:T(1,128)} %bitcast.6), calls=%async_computation | async-start | bytes 8192 | tf_op jit(solution)/shard_map/all_to_all | solution.py:69
  15.3 3.4 %scatter_fusion = bf16[64,64,128]{2,1,0:T(8,128)(2,1)S(1)} fusion(bf16[64,64,128]{2,1,0:T(8,128)(2,1)S(1)} %broadcast_in_dim.90, s32[32]{0:T(128)S(1)} %fusion.44, bf16[32,64,128]{2,1,0:T(8,128)(2,1)} %bitcast.120), kind=kCustom, calls=%fused_computation.2 | custom fusion | bytes 1572992 | tf_op jit(solution)/shard_map/scatter | solution.py:59
  18.7 1.7 copy.28
  20.4 4.2 %all-to-all-start.1 = ((bf16[8,8,64,128]{3,1,2,0:T(8,128)(2,1)}), bf16[8,8,64,128]{3,1,2,0:T(8,128)(2,1)S(1)}, u32[]{:S(2)}, u32[]{:S(2)}) async-start(bf16[8,8,64,128]{3,1,2,0:T(8,128)(2,1)} %copy.28), calls=%async_computation.1 | async-start | bytes 2097152 | tf_op jit(solution)/shard_map/all_to_all | solution.py:62
  27.4 12.6 %all-to-all-done.1 = bf16[8,8,64,128]{3,1,2,0:T(8,128)(2,1)S(1)} async-done(((bf16[8,8,64,128]{3,1,2,0:T(8,128)(2,1)}), bf16[8,8,64,128]{3,1,2,0:T(8,128)(2,1)S(1)}, u32[]{:S(2)}, u32[]{:S(2)}) %all-to-all-start.1) | async-done | bytes 1048608 | tf_op jit(solution)/shard_map/all_to_all | solution.py:62
  42.7 1.6 copy.49
  44.3 2.7 %copy.32 = f32[640,640]{0,1:T(8,128)} copy(f32[640,640]{1,0:T(8,128)} %bitcast.118) | data formatting | bytes 3276800 | tf_op jit(solution)/shard_map/reshape | solution.py:33
  47.0 2.0 fusion.7
  49.5 1.3 slice.135
  51.1 1.7 copy.33
  54.0 11.7 %cholesky.104 = f32[128,128]{1,0:T(8,128)S(1)} custom-call(f32[128,128]{1,0:T(8,128)S(1)} %cholesky.266), custom_call_target="Cholesky" | custom-call | tf_op jit(solution)/shard_map/jit(cholesky)/cholesky | solution.py:36
  65.7 9.8 %custom-call.31 = f32[1,128,128]{1,2,0:T(8,128)S(1)} custom-call(f32[1,128,128]{2,1,0:T(8,128)S(1)} %get-tuple-element.36), custom_call_target="InvertDiagBlocksLowerTriangular" | custom-call | tf_op jit(solution)/shard_map/jit(cholesky)/cholesky | solution.py:36
  75.7 1.2 constant_dynamic-update-slice_fusion.3
  76.9 1.3 convolution_subtract_fusion
  78.2 11.7 %cholesky.217 = f32[128,128]{1,0:T(8,128)S(1)} custom-call(f32[128,128]{1,0:T(8,128)S(1)} %cholesky.270), custom_call_target="Cholesky" | custom-call | tf_op jit(solution)/shard_map/jit(cholesky)/cholesky | solution.py:36
  89.9 9.9 %custom-call.32 = f32[1,128,128]{1,2,0:T(8,128)S(1)} custom-call(f32[1,128,128]{2,1,0:T(8,128)S(1)} %get-tuple-element.33), custom_call_target="InvertDiagBlocksLowerTriangular" | custom-call | tf_op jit(solution)/shard_map/jit(cholesky)/cholesky | solution.py:36
  100.1 1.3 convolution_subtract_fusion.1
  101.4 11.7 %cholesky.238 = f32[128,128]{1,0:T(8,128)S(1)} custom-call(f32[128,128]{1,0:T(8,128)S(1)} %cholesky.275), custom_call_target="Cholesky" | custom-call | tf_op jit(solution)/shard_map/jit(cholesky)/cholesky | solution.py:36
  113.9 9.8 %custom-call.33 = f32[1,128,128]{1,2,0:T(8,128)S(1)} custom-call(f32[1,128,128]{2,1,0:T(8,128)S(1)} %get-tuple-element.30), custom_call_target="InvertDiagBlocksLowerTriangular" | custom-call | tf_op jit(solution)/shard_map/jit(cholesky)/cholesky | solution.py:36
  123.9 1.2 convolution_subtract_fusion.5
  125.1 11.9 %cholesky.255 = f32[128,128]{1,0:T(8,128)S(1)} custom-call(f32[128,128]{1,0:T(8,128)S(1)} %convolution_subtract_fusion.5), custom_call_target="Cholesky" | custom-call | tf_op jit(solution)/shard_map/jit(cholesky)/cholesky | solution.py:36
  141.2 10.4 %while.1 = (s32[]{:T(128)}, f32[512,512]{1,0:T(8,128)S(1)}, s32[4,2]{0,1:T(2,128)S(1)}, f32[4,128,128]{2,1,0:T(8,128)}, s32[]{:T(128)}) while((s32[]{:T(128)}, f32[512,512]{1,0:T(8,128)S(1)}, s32[4,2]{0,1:T(2,128)S(1)}, f32[4,128,128]{2,1,0:T(8,128)}, s32[]{:T(128)}) %tuple.35), condition=%wide.while_cond, body=%wide.while_body.sunk | while | flops 2 | bytes 132705 | solution.py:37
  141.8 2.0 bitcast_dynamic-update-slice_fusion.2
  144.4 2.0 bitcast_dynamic-update-slice_fusion.2
  147.0 2.0 bitcast_dynamic-update-slice_fusion.2
  149.6 2.0 bitcast_dynamic-update-slice_fusion.2
  151.6 40.1 %custom-call.34 = f32[4,128,128]{1,2,0:T(8,128)S(1)} custom-call(f32[4,128,128]{2,1,0:T(8,128)} %get-tuple-element.9), custom_call_target="InvertDiagBlocksLowerTriangular" | custom-call | tf_op jit(solution)/shard_map/jit(_solve_triangular)/triangular_solve | solution.py:37
  194.5 2.6 %collective-permute-start.1 = (f32[1,128,128]{2,1,0:T(8,128)S(1)}, f32[1,128,128]{2,1,0:T(8,128)S(1)}, u32[]{:S(2)}, u32[]{:S(2)}) collective-permute-start(f32[1,128,128]{2,1,0:T(8,128)S(1)} %get-tuple-element.26), channel_id=1, source_target_pairs={{0,7},{1,0},{2,1},{3,2},{4,3},{5,4},{6,5},{7,6},{8,15},{9,8},{10,9... | collective-permute-start | bytes 196616 | tf_op jit(solution)/shard_map/ppermute | solution.py:12
  197.7 2.0 collective-permute-done
  199.7 1.6 collective-permute-done.2
  203.2 32.7 %all-reduce.3.cloned.1.call-done = f32[1,128,128]{2,1,0:T(8,128)} async-done(((f32[1,128,128]{2,1,0:T(8,128)}), f32[1,128,128]{2,1,0:T(8,128)}) %all-reduce.3.cloned.1.call-update) | async-done | bytes 65552 | tf_op jit(solution)/shard_map/psum | solution.py:86
  235.9 1.5 copy.66
  (87 shorter events, 20.0 us)
Async XLA Ops:
  9.8 10.6 %all-to-all-start = ((s32[8,1,8]{2,1,0:T(1,128)}), s32[8,1,8]{2,1,0:T(1,128)S(1)}, u32[]{:S(2)}, u32[]{:S(2)}) async-start(s32[8,1,8]{2,1,0:T(1,128)} %bitcast.6), calls=%async_computation | async-start | bytes 8192 | tf_op jit(solution)/shard_map/all_to_all | solution.py:69
  18.7 6.0 %copy-start.6 = (s32[1,8]{1,0:T(1,128)S(1)}, s32[1,8]{1,0:T(1,128)}, u32[]{:S(2)}) copy-start(s32[1,8]{1,0:T(1,128)} %param.13) | copy-start | bytes 100
  18.7 6.0 %copy-start.7 = (s32[1,8]{1,0:T(1,128)S(1)}, s32[1,8]{1,0:T(1,128)}, u32[]{:S(2)}) copy-start(s32[1,8]{1,0:T(1,128)} %param.12) | copy-start | bytes 100
  18.7 7.3 %copy-start.8 = (s32[50]{0:T(128)S(1)}, s32[50]{0:T(128)}, u32[]{:S(2)}) copy-start(s32[50]{0:T(128)} %constant.222) | copy-start | bytes 604
  18.7 7.3 %copy-start.4 = (f32[1,8,640]{2,1,0:T(8,128)S(1)}, f32[1,8,640]{2,1,0:T(8,128)}, u32[]{:S(2)}) copy-start(f32[1,8,640]{2,1,0:T(8,128)} %param.14) | copy-start | bytes 61444
  20.4 19.6 %all-to-all-start.1 = ((bf16[8,8,64,128]{3,1,2,0:T(8,128)(2,1)}), bf16[8,8,64,128]{3,1,2,0:T(8,128)(2,1)S(1)}, u32[]{:S(2)}, u32[]{:S(2)}) async-start(bf16[8,8,64,128]{3,1,2,0:T(8,128)(2,1)} %copy.28), calls=%async_computation.1 | async-start | bytes 2097152 | tf_op jit(solution)/shard_map/all_to_all | solution.py:62
  24.6 211.2 %all-reduce.3.cloned.1.call-start = ((), (), s32[]{:S(2)}) async-start(), calls=%async_computation.2 | async-start | bytes 131072 | tf_op jit(solution)/shard_map/psum | solution.py:86
  40.9 0.7 copy-start.5
  47.0 2.0 copy-start
  49.5 1.5 copy-start.1
  51.1 1.7 copy-start.2
  53.0 1.0 copy-start.3
  194.4 5.3 %collective-permute-start = (f32[1,128,128]{2,1,0:T(8,128)S(1)}, f32[1,128,128]{2,1,0:T(8,128)S(1)}, u32[]{:S(2)}, u32[]{:S(2)}) collective-permute-start(f32[1,128,128]{2,1,0:T(8,128)S(1)} %get-tuple-element.24), channel_id=1, source_target_pairs={{0,1},{1,2},{2,3},{3,4},{4,5},{5,6},{6,7},{7,0},{8,9},{9,10},{10,1... | collective-permute-start | bytes 196616 | tf_op jit(solution)/shard_map/ppermute | solution.py:12
  194.5 5.3 %collective-permute-start.1 = (f32[1,128,128]{2,1,0:T(8,128)S(1)}, f32[1,128,128]{2,1,0:T(8,128)S(1)}, u32[]{:S(2)}, u32[]{:S(2)}) collective-permute-start(f32[1,128,128]{2,1,0:T(8,128)S(1)} %get-tuple-element.26), channel_id=1, source_target_pairs={{0,7},{1,0},{2,1},{3,2},{4,3},{5,4},{6,5},{7,6},{8,15},{9,8},{10,9... | collective-permute-start | bytes 196616 | tf_op jit(solution)/shard_map/ppermute | solution.py:12
  197.1 4.3 %collective-permute-start.2 = (f32[1,128,128]{2,1,0:T(8,128)S(1)}, f32[1,128,128]{2,1,0:T(8,128)S(1)}, u32[]{:S(2)}, u32[]{:S(2)}) collective-permute-start(f32[1,128,128]{2,1,0:T(8,128)S(1)} %get-tuple-element.25), channel_id=1, source_target_pairs={{0,4},{1,5},{2,6},{3,7},{4,0},{5,1},{6,2},{7,3},{8,12},{9,13},{10,... | collective-permute-start | bytes 196616 | tf_op jit(solution)/shard_map/ppermute | solution.py:12
Sparse Core Ops, SparseCore 0:
  202.1 33.6 all-reduce.2
where the time goes:
time: 245 us; the launch traced here: 244 us
  other arithmetic  126 us (51%)
  waiting for transfers between devices  49 us (20%)
  local copies, waits for them, and re-layouts  30.5 us (12%)
  between operations  17.7 us (7%)
  starting transfers between devices  12.7 us (5%)
  matrix products  8.06 us (3%)
    another operation x14, other arithmetic, front_factor(): jnp.linalg.cholesky(front_matrix[:elimination_count, :elimination_count])  78.7 us
    another operation x3, other arithmetic, front_factor(): jax.scipy.linalg.solve_triangular(lower_triangle, front_matrix[eliminatio...  40.4 us
    psum x1, waiting for transfers between devices, body(): total = lax.psum(local_sum, 'grp')  32.7 us
    all_to_all x1, waiting for transfers between devices, body(): lax.all_to_all(outgoing.reshape(width, room, rows, column_indices), 'sep'...  12.6 us
    another operation x12, local copies, waits for them, and re-layouts  10.4 us
    another operation x6, matrix products, front_factor(): jnp.linalg.cholesky(front_matrix[:elimination_count, :elimination_count])  5.47 us
    all_to_all x1, starting transfers between devices, body(): lax.all_to_all(labels.reshape(width, room), 'sep', split_axis=0, concat_a...  5.2 us
  transfers between devices with their start and end apart: 6, of which 4 were waited for; matrix products, arithmetic and copies ran while one was open for 3% of the time, Pallas kernels for 0%

commit v1 on v0

v1 whole, which is shorter than its diff:
```python
import functools
import jax
import jax.numpy as jnp
from jax import lax
from jax.experimental import pallas as pl
from jax.experimental.pallas import tpu as pltpu
from jax.sharding import PartitionSpec as P

MESH = pl.DeviceIdType.MESH

PANEL = 8


def dot_nt(a, b):
    return lax.dot_general(a, b, (((1,), (1,)), ((), ())), precision=lax.Precision.HIGHEST, preferred_element_type=jnp.float32)


def lanes(x, j):
    return jnp.broadcast_to(x[:, j : j + 1], x.shape)


def sublanes(x, r):
    return jnp.broadcast_to(x[r : r + 1, :], x.shape)


def factor_diagonal(a_ref, u_ref, w_ref):
    size = a_ref.shape[0]
    panels = size // PANEL
    sub = lax.broadcasted_iota(jnp.int32, (PANEL, size), 0)
    lane = lax.broadcasted_iota(jnp.int32, (PANEL, size), 1)
    a = [a_ref[PANEL * i : PANEL * (i + 1), :] for i in range(panels)]
    w = [jnp.where(lane == sub + PANEL * i, 1.0, 0.0) for i in range(panels)]
    for p in range(panels):
        j0 = PANEL * p
        cols = [lanes(a[p], j0 + r) for r in range(PANEL)]
        b = [[sublanes(cols[r], s) for s in range(r + 1)] for r in range(PANEL)]
        ta = [sublanes(a[p], r) for r in range(PANEL)]
        tw = [sublanes(w[p], r) for r in range(PANEL)]
        inv = [None] * PANEL
        n = [[None] * PANEL for _ in range(PANEL)]
        for r in range(PANEL):
            inv[r] = 1.0 / b[r][r]
            for s in range(r + 1, PANEL):
                n[s][r] = b[s][r] * inv[r]
            for s in range(r + 1, PANEL):
                for t in range(r + 1, s + 1):
                    b[s][t] = b[s][t] - n[s][r] * b[t][r]
            for s in range(r + 1, PANEL):
                ta[s] = ta[s] - n[s][r] * ta[r]
                tw[s] = tw[s] - n[s][r] * tw[r]
        u = ta[0] * lax.rsqrt(b[0][0])
        v = tw[0] * lax.rsqrt(b[0][0])
        for r in range(1, PANEL):
            root = lax.rsqrt(b[r][r])
            u = jnp.where(sub == r, ta[r] * root, u)
            v = jnp.where(sub == r, tw[r] * root, v)
        u_ref[j0 : j0 + PANEL, :] = jnp.where(lane >= sub + j0, u, 0.0)
        w_ref[j0 : j0 + PANEL, :] = v
        if p + 1 < panels:
            ya = [None] * PANEL
            yw = [None] * PANEL
            for r in reversed(range(PANEL)):
                ya[r] = ta[r] * inv[r]
                yw[r] = tw[r] * inv[r]
            for r in reversed(range(PANEL)):
                for s in range(r):
                    ya[s] = ya[s] - n[r][s] * ya[r]
                    yw[s] = yw[s] - n[r][s] * yw[r]
            for i in range(p + 1, panels):
                for s in range(PANEL):
                    c = lanes(a[i], j0 + s)
                    a_new = c * ya[s] if s == 0 else a_new + c * ya[s]
                    w_new = c * yw[s] if s == 0 else w_new + c * yw[s]
                a[i] = a[i] - a_new
                w[i] = w[i] - w_new


def front_kernel(rows, offsets, codes, distance, tiles, pivots, factor_ref, pieces_ref, acc, diag, up, winv, schur_ref):
    size = tiles.shape[2]
    blocks = pivots.shape[0]
    elim = blocks - 1
    acc[...] = jnp.zeros_like(acc)

    def add_tile(t, carry):
        code = codes[t]
        c = code & 7
        r = pl.multiple_of((code >> 3) * rows, rows)
        acc[c, pl.ds(r, rows), :] += tiles[t].astype(jnp.float32)
        return carry

    lax.fori_loop(0, tiles.shape[0], add_tile, 0, unroll=4)

    sub = lax.broadcasted_iota(jnp.int32, (size, size), 0)
    lane = lax.broadcasted_iota(jnp.int32, (size, size), 1)

    def span(i):
        return slice(i * size, (i + 1) * size)

    row_sums = [jnp.zeros((size, 1), jnp.float32) for _ in range(blocks)]
    for j in range(elim):
        f = acc[j, span(j), :]
        mixed = jnp.where(sub == lane, 0.0, 0.5 * (f + f.T))
        sums = pivots[j : j + 1, :] + jnp.sum(mixed, 0, keepdims=True)
        for i in range(j + 1, blocks):
            half = 0.5 * acc[j, span(i), :]
            sums = sums + jnp.sum(half, 0, keepdims=True)
            if i < elim:
                row_sums[i] = row_sums[i] + jnp.sum(half, 1, keepdims=True)
            acc[j, span(i), :] = -half
        acc[j, span(j), :] = jnp.where(sub == lane, sums + row_sums[j], -mixed)

    def step(k, carry):
        diag[...] = acc[k, pl.ds(pl.multiple_of(k * size, size), size), :]
        factor_diagonal(diag, up, winv)
        for kk in range(elim):
            @pl.when(k == kk)
            def _():
                w = winv[...]
                factor_ref[span(kk), span(kk)] = up[...].T
                for j in range(kk + 1, elim):
                    factor_ref[span(kk), span(j)] = jnp.zeros((size, size), jnp.float32)
                below = dot_nt(acc[kk, (kk + 1) * size : blocks * size, :], w)
                factor_ref[(kk + 1) * size : blocks * size, span(kk)] = below
                for j in range(kk + 1, elim):
                    o = (j - kk - 1) * size
                    acc[j, j * size : blocks * size, :] -= dot_nt(below[o:, :], below[o : o + size, :])
                last = below[(elim - kk - 1) * size :, :]
                if kk == 0:
                    schur_ref[...] = dot_nt(last, last)
                else:
                    schur_ref[...] += dot_nt(last, last)
        return carry

    lax.fori_loop(0, elim, step, 0)
    for n, offset in enumerate(offsets):
        pieces_ref[n] = jnp.where(distance[0] == offset, schur_ref[...], 0.0)


def front_call(codes, distance, tiles, pivots, rows, columns, offsets):
    blocks = pivots.shape[0]
    return pl.pallas_call(
        functools.partial(front_kernel, rows, offsets),
        out_shape=(
            jax.ShapeDtypeStruct((blocks * columns, (blocks - 1) * columns), jnp.float32),
            jax.ShapeDtypeStruct((len(offsets), columns, columns), jnp.float32),
        ),
        in_specs=[
            pl.BlockSpec(memory_space=pltpu.SMEM),
            pl.BlockSpec(memory_space=pltpu.SMEM),
            pl.BlockSpec(memory_space=pltpu.VMEM),
            pl.BlockSpec(memory_space=pltpu.VMEM),
        ],
        out_specs=(pl.BlockSpec(memory_space=pltpu.VMEM), pl.BlockSpec(memory_space=pltpu.VMEM)),
        scratch_shapes=[
            pltpu.VMEM((blocks, blocks * columns + rows, columns), jnp.float32),
            pltpu.VMEM((columns, columns), jnp.float32),
            pltpu.VMEM((columns, columns), jnp.float32),
            pltpu.VMEM((columns, columns), jnp.float32),
            pltpu.VMEM((columns, columns), jnp.float32),
        ],
    )(codes, distance, tiles, pivots)


def schur_kernel(groups, width, offsets, pieces, total, arrived, gathered, send1, recv1, send2, recv2):
    grp = lax.axis_index("grp")
    sep = lax.axis_index("sep")
    barrier = pltpu.get_barrier_semaphore()
    for offset in offsets[1:]:
        pl.semaphore_signal(barrier, inc=1, device_id=(grp, (sep + offset) % width), device_id_type=MESH)
    for hop in range(1, groups):
        pl.semaphore_signal(barrier, inc=1, device_id=((grp + hop) % groups, sep), device_id_type=MESH)
    pl.semaphore_wait(barrier, len(offsets) - 1 + groups - 1)
    first = []
    for n, offset in enumerate(offsets[1:]):
        copy = pltpu.make_async_remote_copy(
            src_ref=pieces.at[n + 1],
            dst_ref=arrived.at[n],
            send_sem=send1.at[n],
            recv_sem=recv1.at[n],
            device_id=(grp, (sep + offset) % width),
            device_id_type=MESH,
        )
        copy.start()
        first.append(copy)
    for copy in first:
        copy.wait_recv()
    local = pieces[0]
    for n in range(len(first)):
        local = local + arrived[n]
    gathered[grp] = local
    second = []
    for hop in range(1, groups):
        copy = pltpu.make_async_remote_copy(
            src_ref=gathered.at[grp],
            dst_ref=gathered.at[grp],
            send_sem=send2.at[hop - 1],
            recv_sem=recv2.at[hop - 1],
            device_id=((grp + hop) % groups, sep),
            device_id_type=MESH,
        )
        copy.start()
        second.append(copy)
    for copy in first:
        copy.wait_send()
    for copy in second:
        copy.wait_recv()
    summed = gathered[0]
    for g in range(1, groups):
        summed = summed + gathered[g]
    total[...] = summed
    for copy in second:
        copy.wait_send()


def schur_call(pieces, groups, width, offsets):
    _, size, _ = pieces.shape
    partners = len(offsets) - 1
    return pl.pallas_call(
        functools.partial(schur_kernel, groups, width, offsets),
        out_shape=jax.ShapeDtypeStruct((size, size), jnp.float32),
        in_specs=[pl.BlockSpec(memory_space=pltpu.VMEM)],
        out_specs=pl.BlockSpec(memory_space=pltpu.VMEM),
        scratch_shapes=[
            pltpu.VMEM((partners, size, size), jnp.float32),
            pltpu.VMEM((groups, size, size), jnp.float32),
            pltpu.SemaphoreType.DMA((partners,)),
            pltpu.SemaphoreType.DMA((partners,)),
            pltpu.SemaphoreType.DMA((groups - 1,)),
            pltpu.SemaphoreType.DMA((groups - 1,)),
        ],
        compiler_params=pltpu.CompilerParams(collective_id=1, has_side_effects=True),
    )(pieces)


def position_codes(positions, rows, columns):
    ratio = columns // rows
    row_count = 5 * ratio
    starts = [0]
    for r in range(row_count):
        starts.append(starts[-1] + r // ratio + 1)
    row = sum((positions >= starts[r]).astype(jnp.int32) for r in range(1, row_count))
    begin = sum(jnp.where(positions >= starts[r], starts[r] - starts[r - 1], 0) for r in range(1, row_count))
    return row * 8 + positions - begin, row_count * 8


def body(groups, width, tiles, tile_front, tile_pos, front_slot, front_parent, pivot):
    myself = lax.axis_index("sep")
    held = tiles.shape[1]
    rows = tiles.shape[2]
    columns = tiles.shape[3]
    fronts = front_slot.shape[1]
    room = max(2, -(-2 * held // width))
    offsets = (0, 1, width - 1, width // 2)
    slots = front_slot[0]
    parents = front_parent[0]
    front_ids = jnp.arange(fronts, dtype=jnp.int32)
    owner_of = jnp.sum(jnp.where(tile_front[0] == front_ids[None, :], slots[None, :], 0), 1)
    target = (owner_of[:, None] == jnp.arange(width, dtype=jnp.int32)[None, :]).astype(jnp.int32)
    rank = jnp.sum(target * (jnp.cumsum(target, 0) - 1), 1)
    place = owner_of * room + rank
    codes, empty = position_codes(tile_pos[0], rows, columns)
    outgoing = jnp.zeros((width * room, rows, columns), jnp.bfloat16).at[place].set(tiles[0])
    labels = jnp.full((width * room,), empty, jnp.int32).at[place].set(codes)
    arrived, labels = (
        lax.all_to_all(outgoing.reshape(width, room, rows, columns), "sep", split_axis=0, concat_axis=0, tiled=True),
        lax.all_to_all(labels.reshape(width, room), "sep", split_axis=0, concat_axis=0, tiled=True),
    )
    arrived = arrived.reshape(width * room, rows, columns)
    labels = labels.reshape(width * room)
    mine = slots == myself
    pivots = jnp.sum(jnp.where(mine[:, None], pivot[0], 0.0), 0).reshape(-1, columns)
    parent = jnp.sum(jnp.where(mine, parents, 0))
    distance = jnp.reshape((parent - myself) % width, (1,))
    factor, pieces = front_call(labels, distance, arrived, pivots, rows, columns, offsets)
    total = schur_call(pieces, groups, width, offsets)
    return (factor[None, None], total[None])


def solution(mesh):
    placed = (
        P("grp", "sep", None, None),
        P("grp", "sep", None),
        P("grp", "sep"),
        P("grp", None),
        P("grp", None),
        P("grp", None, None),
    )
    return jax.shard_map(
        functools.partial(body, mesh.shape["grp"], mesh.shape["sep"]),
        mesh=mesh,
        in_specs=placed,
        out_specs=(P("grp", "sep", None, None), P("sep", None, None)),
        check_vma=False,
    )
```

time: 245 us -> 77.2 us (0.32)
  other arithmetic: 126 us -> 3.9 us
  Pallas kernels: 0 us -> 39.7 us
  waiting for transfers between devices: 49 us -> 11.5 us
  local copies, waits for them, and re-layouts: 30.5 us -> 10.6 us
  between operations: 17.7 us -> 1.37 us
  matrix products: 8.06 us -> 0 us
  starting transfers between devices: 12.7 us -> 9.54 us
    another operation x17 -> x0, other arithmetic: 119 us -> none  [the longest x14 78.7 us: front_factor(): jnp.linalg.cholesky(front_matrix[:elimination_count, :elimination_count])]
    pallas_call x0 -> x2, Pallas kernels: none -> 39.7 us  [the longest x1 25.4 us: front_call(): pl.pallas_call(functools.partial(front_kernel, rows, offsets), out_shape=...]
    psum x1 -> x0, waiting for transfers between devices: 32.7 us -> none  [body(): total = lax.psum(local_sum, 'grp')]
    another operation x20 -> x0, local copies, waits for them, and re-layouts: 10.8 us -> none
    another operation x13 -> x0, matrix products: 7.39 us -> none  [the longest x6 5.47 us: front_factor(): jnp.linalg.cholesky(front_matrix[:elimination_count, :elimination_count])]
    reshape x2 -> x1, local copies, waits for them, and re-layouts: 4.43 us -> 0.6 us  [body(): labels = labels.reshape(width * room)]
    ppermute x3 -> x0, waiting for transfers between devices: 3.67 us -> none  [passed_along(): lax.ppermute(shard, axis, [(i, (i + by) % devices) for i in range(devices)])]
    ppermute x3 -> x0, starting transfers between devices: 3.26 us -> none  [passed_along(): lax.ppermute(shard, axis, [(i, (i + by) % devices) for i in range(devices)])]
  transfers between devices with their start and end apart: 6 -> 2, of which waited for: 4 -> 1; matrix products, arithmetic and copies ran while one was open for 3% -> 11% of each run, Pallas kernels for 0% -> 0%
where the time goes in v1:
time: 77.2 us; the launch traced here: 76.6 us
  Pallas kernels  39.7 us (51%)
  waiting for transfers between devices  11.5 us (15%)
  local copies, waits for them, and re-layouts  10.6 us (14%)
  starting transfers between devices  9.54 us (12%)
  other arithmetic  3.9 us (5%)
  between operations  1.37 us (2%)
    pallas_call x1, Pallas kernels, front_call(): pl.pallas_call(functools.partial(front_kernel, rows, offsets), out_shape=...  25.4 us
    pallas_call x1, Pallas kernels, schur_call(): pl.pallas_call(functools.partial(schur_kernel, groups, width, offsets), o...  14.3 us
    all_to_all x1, waiting for transfers between devices, body(): lax.all_to_all(outgoing.reshape(width, room, rows, columns), 'sep', split...  11.5 us
    all_to_all x1, starting transfers between devices, body(): lax.all_to_all(labels.reshape(width, room), 'sep', split_axis=0, concat_a...  5.2 us
    scatter x1, local copies, waits for them, and re-layouts, body(): jnp.zeros((width * room, rows, columns), jnp.bfloat16).at[place]  4.35 us
    all_to_all x1, starting transfers between devices, body(): lax.all_to_all(outgoing.reshape(width, room, rows, columns), 'sep', split...  4.34 us
    unnamed x11, local copies, waits for them, and re-layouts  2.48 us
  transfers between devices with their start and end apart: 2, of which 1 were waited for; matrix products, arithmetic and copies ran while one was open for 11% of the time, Pallas kernels for 0%

profile of v1, /device:TPU:0, one launch (start us, length us, event | category | flops | bytes accessed | tf_op | source)
XLA Modules:
  0.0 76.6 jit_solution(18054122884874184760)
XLA Ops:
  0.6 0.0 copy-start.1
  0.6 0.7 fusion.18
  1.4 0.8 %select_reduce_fusion.1 = s32[32]{0:T(128)S(1)} fusion(s32[8]{0:T(128)} %bitcast.32, s32[32]{0:T(128)} %bitcast.34), kind=kLoop, calls=%fused_computation.7 | loop fusion | flops 736 | bytes 288 | tf_op jit(solution)/shard_map/reduce_sum | solution.py:257
  2.2 0.1 fusion.1
  2.3 0.1 reduce_window_sum.11
  2.3 0.2 select_reduce_fusion
  2.5 0.7 scatter_custom_fusion
  3.2 0.7 all_to_all.9
  3.9 5.2 %all-to-all-start = ((s32[8,1,8]{2,1,0:T(1,128)}), s32[8,1,8]{2,1,0:T(1,128)S(1)}, u32[]{:S(2)}, u32[]{:S(2)}) async-start(s32[8,1,8]{2,1,0:T(1,128)} %bitcast.5), calls=%async_computation | async-start | bytes 8192 | tf_op jit(solution)/shard_map/all_to_all | solution.py:266
  9.1 1.2 %broadcast_in_dim.79 = bf16[64,64,128]{2,1,0:T(8,128)(2,1)} broadcast(bf16[]{:T(256)} %constant.58.clone.1), dimensions={} | broadcast | bytes 1048578 | tf_op jit(solution)/shard_map/broadcast_in_dim | solution.py:262
  10.3 0.0 copy-done.1
  10.3 4.4 %scatter_fusion = bf16[64,64,128]{2,1,0:T(8,128)(2,1)} fusion(bf16[64,64,128]{2,1,0:T(8,128)(2,1)} %broadcast_in_dim.79, s32[32]{0:T(128)S(1)} %fusion.21, bf16[32,64,128]{2,1,0:T(8,128)(2,1)S(1)} %bitcast.29), kind=kCustom, calls=%fused_computation.1 | custom fusion | bytes 1572992 | tf_op jit(solution)/shard_map/scatter | solution.py:262
  14.7 0.0 copy-start.3
  14.7 0.0 copy-start.4
  14.7 0.0 copy-start.2
  14.7 0.0 all-to-all-done
  14.7 4.3 %all-to-all-start.1 = ((bf16[8,8,64,128]{3,2,1,0:T(8,128)(2,1)}), bf16[8,8,64,128]{3,2,1,0:T(8,128)(2,1)S(1)}, u32[]{:S(2)}, u32[]{:S(2)}) async-start(bf16[8,8,64,128]{3,2,1,0:T(8,128)(2,1)} %bitcast.9), calls=%async_computation.1 | async-start | bytes 2097152 | tf_op jit(solution)/shard_map/all_to_all | solution.py:265
  19.0 0.0 copy-done.3
  19.0 0.0 copy-done.4
  19.1 0.6 fusion.22
  20.4 0.0 copy-done.2
  20.4 0.7 fusion
  21.0 0.6 broadcast.103
  21.6 0.7 reduce.3
  22.3 0.6 reshape.57.codes
  22.9 11.5 %all-to-all-done.1 = bf16[8,8,64,128]{3,2,1,0:T(8,128)(2,1)S(1)} async-done(((bf16[8,8,64,128]{3,2,1,0:T(8,128)(2,1)}), bf16[8,8,64,128]{3,2,1,0:T(8,128)(2,1)S(1)}, u32[]{:S(2)}, u32[]{:S(2)}) %all-to-all-start.1) | async-done | bytes 1048608 | tf_op jit(solution)/shard_map/all_to_all | solution.py:265
  34.4 0.0 copy-start
  34.4 1.0 %copy-done = bf16[8,8,64,128]{3,2,1,0:T(8,128)(2,1)} copy-done((bf16[8,8,64,128]{3,2,1,0:T(8,128)(2,1)}, bf16[8,8,64,128]{3,2,1,0:T(8,128)(2,1)S(1)}, u32[]{:S(2)}) %copy-start) | copy-done | bytes 1048600
  35.4 25.4 %shard_map.77 = (f32[640,512]{1,0:T(8,128)}, f32[4,128,128]{2,1,0:T(8,128)}) custom-call(s32[64]{0:T(128)} %reshape.57.codes, s32[1]{0:T(128)} %bitcast.7.distance, bf16[64,64,128]{2,1,0:T(8,128)(2,1)} %bitcast.28, f32[5,128]{1,0:T(8,128)} %bitcast.31), custom_call_target="tpu_custom_call" | custom-call | tf_op jit(solution)/shard_map/pallas_call | solution.py:141
  60.8 14.3 %shard_map.78 = f32[128,128]{1,0:T(8,128)} custom-call(f32[4,128,128]{2,1,0:T(8,128)} %get-tuple-element.5.pieces), custom_call_target="tpu_custom_call" | custom-call | tf_op jit(solution)/shard_map/pallas_call | solution.py:218
  75.1 1.5 %copy.11 = f32[1,128,128]{2,1,0:T(8,128)} copy(f32[1,128,128]{2,1,0:T(8,128)} %bitcast.30) | data formatting | bytes 131072
  (1 shorter events, 0.0 us)
Async XLA Ops:
  0.6 9.7 %copy-start.1 = (bf16[1,32,64,128]{3,2,1,0:T(8,128)(2,1)S(1)}, bf16[1,32,64,128]{3,2,1,0:T(8,128)(2,1)}, u32[]{:S(2)}) copy-start(bf16[1,32,64,128]{3,2,1,0:T(8,128)(2,1)} %param.6) | copy-start | bytes 1572868
  3.9 10.8 %all-to-all-start = ((s32[8,1,8]{2,1,0:T(1,128)}), s32[8,1,8]{2,1,0:T(1,128)S(1)}, u32[]{:S(2)}, u32[]{:S(2)}) async-start(s32[8,1,8]{2,1,0:T(1,128)} %bitcast.5), calls=%async_computation | async-start | bytes 8192 | tf_op jit(solution)/shard_map/all_to_all | solution.py:266
  14.7 4.4 %copy-start.3 = (s32[1,8]{1,0:T(1,128)S(1)}, s32[1,8]{1,0:T(1,128)}, u32[]{:S(2)}) copy-start(s32[1,8]{1,0:T(1,128)} %param.9) | copy-start | bytes 100
  14.7 4.4 %copy-start.4 = (s32[1,8]{1,0:T(1,128)S(1)}, s32[1,8]{1,0:T(1,128)}, u32[]{:S(2)}) copy-start(s32[1,8]{1,0:T(1,128)} %param.10) | copy-start | bytes 100
  14.7 5.7 %copy-start.2 = (f32[1,8,640]{2,1,0:T(8,128)S(1)}, f32[1,8,640]{2,1,0:T(8,128)}, u32[]{:S(2)}) copy-start(f32[1,8,640]{2,1,0:T(8,128)} %param.11) | copy-start | bytes 61444
  14.7 19.7 %all-to-all-start.1 = ((bf16[8,8,64,128]{3,2,1,0:T(8,128)(2,1)}), bf16[8,8,64,128]{3,2,1,0:T(8,128)(2,1)S(1)}, u32[]{:S(2)}, u32[]{:S(2)}) async-start(bf16[8,8,64,128]{3,2,1,0:T(8,128)(2,1)} %bitcast.9), calls=%async_computation.1 | async-start | bytes 2097152 | tf_op jit(solution)/shard_map/all_to_all | solution.py:265
  34.4 1.0 %copy-start = (bf16[8,8,64,128]{3,2,1,0:T(8,128)(2,1)}, bf16[8,8,64,128]{3,2,1,0:T(8,128)(2,1)S(1)}, u32[]{:S(2)}) copy-start(bf16[8,8,64,128]{3,2,1,0:T(8,128)(2,1)S(1)} %all-to-all-done.1) | copy-start | bytes 3145732

commit v2 on v1

--- a/solution.py
+++ b/solution.py
@@ -9,6 +9,7 @@
 MESH = pl.DeviceIdType.MESH
 
 PANEL = 8
+GRANT = 20 * 1024 * 1024
 
 
 def dot_nt(a, b):
@@ -75,20 +76,32 @@
                 w[i] = w[i] - w_new
 
 
-def front_kernel(rows, offsets, codes, distance, tiles, pivots, factor_ref, pieces_ref, acc, diag, up, winv, schur_ref):
-    size = tiles.shape[2]
-    blocks = pivots.shape[0]
+def front_kernel(offsets, room, slots, parents, labels, tiles, pivots, factor_ref, pieces_ref, codes, acc, diag, up, winv, schur_ref, sem):
+    width, _, rows, size = tiles.shape
+    blocks = acc.shape[0]
     elim = blocks - 1
+    me = lax.axis_index("sep")
+    fetch = pltpu.make_async_copy(labels, codes, sem)
+    fetch.start()
     acc[...] = jnp.zeros_like(acc)
-
-    def add_tile(t, carry):
-        code = codes[t]
-        c = code & 7
-        r = pl.multiple_of((code >> 3) * rows, rows)
-        acc[c, pl.ds(r, rows), :] += tiles[t].astype(jnp.float32)
+    front = 0
+    parent = 0
+    for f in range(pivots.shape[0]):
+        hit = slots[f] == me
+        front = jnp.where(hit, f, front)
+        parent = jnp.where(hit, parents[f], parent)
+    distance = parent - me
+    distance = jnp.where(distance < 0, distance + width, distance)
+    fetch.wait()
+
+    def add_tiles(s, carry):
+        for t in range(room):
+            code = codes[s, 0, t]
+            r = pl.multiple_of((code >> 3) * rows, rows)
+            acc[code & 7, pl.ds(r, rows), :] += tiles[s, t].astype(jnp.float32)
         return carry
 
-    lax.fori_loop(0, tiles.shape[0], add_tile, 0, unroll=4)
+    lax.fori_loop(0, width, add_tiles, 0)
 
     sub = lax.broadcasted_iota(jnp.int32, (size, size), 0)
     lane = lax.broadcasted_iota(jnp.int32, (size, size), 1)
@@ -96,11 +109,12 @@
     def span(i):
         return slice(i * size, (i + 1) * size)
 
+    picked = lax.broadcasted_iota(jnp.int32, (pivots.shape[0], size), 0) == front
     row_sums = [jnp.zeros((size, 1), jnp.float32) for _ in range(blocks)]
     for j in range(elim):
         f = acc[j, span(j), :]
         mixed = jnp.where(sub == lane, 0.0, 0.5 * (f + f.T))
-        sums = pivots[j : j + 1, :] + jnp.sum(mixed, 0, keepdims=True)
+        sums = jnp.sum(jnp.where(picked, pivots[:, span(j)], 0.0), 0, keepdims=True) + jnp.sum(mixed, 0, keepdims=True)
         for i in range(j + 1, blocks):
             half = 0.5 * acc[j, span(i), :]
             sums = sums + jnp.sum(half, 0, keepdims=True)
@@ -132,33 +146,179 @@
         return carry
 
     lax.fori_loop(0, elim, step, 0)
+    half = size // 2
+    sub = lax.broadcasted_iota(jnp.int32, (half, size), 0)
+    lane = lax.broadcasted_iota(jnp.int32, (half, size), 1)
+    top = pltpu.roll(schur_ref[:half, :], half, 1)
+    bottom = schur_ref[half:, :]
+    packed = jnp.where((lane < half) | (lane - half > sub), bottom, top)
+    tail = jnp.sum(jnp.where(lane - half == sub, bottom, 0.0), 0, keepdims=True)
+    tail = jnp.broadcast_to(tail, (8, size))
     for n, offset in enumerate(offsets):
-        pieces_ref[n] = jnp.where(distance[0] == offset, schur_ref[...], 0.0)
-
-
-def front_call(codes, distance, tiles, pivots, rows, columns, offsets):
-    blocks = pivots.shape[0]
+        pieces_ref[n, :half, :] = jnp.where(distance == offset, packed, 0.0)
+        pieces_ref[n, half:, :] = jnp.where(distance == offset, tail, 0.0)
+
+
+def vmem(count):
+    return [pl.BlockSpec(memory_space=pltpu.VMEM)] * count
+
+
+def smem(count):
+    return [pl.BlockSpec(memory_space=pltpu.SMEM)] * count
+
+
+def front_call(slots, parents, labels, tiles, pivots, offsets, room):
+    width, _, rows, columns = tiles.shape
+    order = pivots.shape[1]
+    square = pltpu.VMEM((columns, columns), jnp.float32)
     return pl.pallas_call(
-        functools.partial(front_kernel, rows, offsets),
+        functools.partial(front_kernel, offsets, room),
         out_shape=(
-            jax.ShapeDtypeStruct((blocks * columns, (blocks - 1) * columns), jnp.float32),
-            jax.ShapeDtypeStruct((len(offsets), columns, columns), jnp.float32),
+            jax.ShapeDtypeStruct((order, order - columns), jnp.float32),
+            jax.ShapeDtypeStruct((len(offsets), columns // 2 + 8, columns), jnp.float32),
         ),
-        in_specs=[
-            pl.BlockSpec(memory_space=pltpu.SMEM),
-            pl.BlockSpec(memory_space=pltpu.SMEM),
-            pl.BlockSpec(memory_space=pltpu.VMEM),
-            pl.BlockSpec(memory_space=pltpu.VMEM),
+        in_specs=smem(2) + vmem(3),
+        out_specs=vmem(2),
+        scratch_shapes=[
+            pltpu.SMEM(labels.shape, jnp.int32),
+            pltpu.VMEM((order // columns, order + rows, columns), jnp.float32),
+            square,
+            square,
+            square,
+            square,
+            pltpu.SemaphoreType.DMA,
         ],
-        out_specs=(pl.BlockSpec(memory_space=pltpu.VMEM), pl.BlockSpec(memory_space=pltpu.VMEM)),
-        scratch_shapes=[
-            pltpu.VMEM((blocks, blocks * columns + rows, columns), jnp.float32),
-            pltpu.VMEM((columns, columns), jnp.float32),
-            pltpu.VMEM((columns, columns), jnp.float32),
-            pltpu.VMEM((columns, columns), jnp.float32),
-            pltpu.VMEM((columns, columns), jnp.float32),
-        ],
-    )(codes, distance, tiles, pivots)
+        compiler_params=pltpu.CompilerParams(vmem_limit_bytes=GRANT),
+        name="front",
+    )(slots, parents, labels, tiles, pivots)
+
+
+def position_codes(positions, rows, columns):
+    ratio = columns // rows
+    row_count = 5 * ratio
+    starts = [0]
+    for r in range(row_count):
+        starts.append(starts[-1] + r // ratio + 1)
+    row = sum((positions >= starts[r]).astype(jnp.int32) for r in range(1, row_count))
+    begin = sum(jnp.where(positions >= starts[r], starts[r] - starts[r - 1], 0) for r in range(1, row_count))
+    return jnp.where(positions < 0, row_count * 8, row * 8 + positions - begin)
+
+
+def pack_kernel(fronts, positions, slots, tiles, outgoing, labels, counts):
+    width = outgoing.shape[0]
+    held, rows, columns = tiles.shape
+    labels[...] = jnp.full(labels.shape, -1, jnp.int32)
+    lane = lax.broadcasted_iota(jnp.int32, labels.shape[1:], 1)
+    for d in range(width):
+        counts[d] = 0
+
+    def place(i, carry):
+        owner = slots[fronts[i]]
+        rank = counts[owner]
+        counts[owner] = rank + 1
+        outgoing[owner, rank] = tiles[i]
+        labels[owner] = jnp.where(lane == rank, positions[i], labels[owner])
+        return carry
+
+    lax.fori_loop(0, held, place, 0, unroll=4)
+    labels[...] = position_codes(labels[...], rows, columns)
+
+
+def pack_call(fronts, positions, slots, tiles, width, room):
+    held, rows, columns = tiles.shape
+    return pl.pallas_call(
+        pack_kernel,
+        out_shape=(
+            jax.ShapeDtypeStruct((width, room, rows, columns), tiles.dtype),
+            jax.ShapeDtypeStruct((width, 1, 128), jnp.int32),
+        ),
+        in_specs=smem(3) + vmem(1),
+        out_specs=vmem(2),
+        scratch_shapes=[pltpu.SMEM((width,), jnp.int32)],
+        compiler_params=pltpu.CompilerParams(vmem_limit_bytes=GRANT),
+        name="pack",
+    )(fronts, positions, slots, tiles)
+
+
+def exchange_kernel(width, order, outgoing, labels, arrived, codes, send, recv, lsend, lrecv, own):
+    grp = lax.axis_index("grp")
+    sep = lax.axis_index("sep")
+    barrier = pltpu.get_barrier_semaphore()
+    bits = [1 << b for b in range(width.bit_length() - 1)]
+    if width == 1 << len(bits):
+        partners = [sum(((sep // b) % 2 + (h // b) % 2) % 2 * b for b in bits) for h in order]
+    else:
+        partners = [(sep + h) % width for h in order]
+    for partner in partners:
+        pl.semaphore_signal(barrier, inc=1, device_id=(grp, partner), device_id_type=MESH)
+    mine = pltpu.make_async_copy(outgoing.at[sep], arrived.at[sep], own.at[0])
+    mine.start()
+    named = pltpu.make_async_copy(labels.at[sep], codes.at[sep], own.at[1])
+    named.start()
+    pl.semaphore_wait(barrier, width - 1)
+    copies = []
+    for n, partner in enumerate(partners):
+        for src, dst, s, r in ((outgoing, arrived, send, recv), (labels, codes, lsend, lrecv)):
+            copy = pltpu.make_async_remote_copy(
+                src_ref=src.at[partner],
+                dst_ref=dst.at[sep],
+                send_sem=s.at[n],
+                recv_sem=r.at[n],
+                device_id=(grp, partner),
+                device_id_type=MESH,
+            )
+            copy.start()
+            copies.append(copy)
+    mine.wait()
+    named.wait()
+    for copy in copies:
+        copy.wait()
+
+
+def exchange_call(outgoing, labels):
+    width = outgoing.shape[0]
+    partners = width - 1
+    order = sorted(range(1, width), key=lambda h: (-bin(h >> 1).count("1"), h))
+    return pl.pallas_call(
+        functools.partial(exchange_kernel, width, order),
+        out_shape=(
+            jax.ShapeDtypeStruct(outgoing.shape, outgoing.dtype),
+            jax.ShapeDtypeStruct(labels.shape, labels.dtype),
+        ),
+        in_specs=vmem(2),
+        out_specs=vmem(2),
+        scratch_shapes=[pltpu.SemaphoreType.DMA((partners,))] * 4 + [pltpu.SemaphoreType.DMA((2,))],
+        compiler_params=pltpu.CompilerParams(collective_id=2, has_side_effects=True, vmem_limit_bytes=GRANT),
+        name="exchange",
+    )(outgoing, labels)
+
+
+def unpack_kernel(packed, out):
+    size = packed.shape[1]
+    half = size // 2
+    sub = lax.broadcasted_iota(jnp.int32, (half, size), 0)
+    lane = lax.broadcasted_iota(jnp.int32, (half, size), 1)
+    body = packed[:half, :]
+    top = pltpu.roll(jnp.where((lane >= half) & (lane - half <= sub), body, 0.0), half, 1)
+    bottom = jnp.where((lane < half) | (lane - half > sub), body, 0.0)
+    lower = jnp.concatenate([top, bottom], 0)
+    sub = lax.broadcasted_iota(jnp.int32, (size, size), 0)
+    lane = lax.broadcasted_iota(jnp.int32, (size, size), 1)
+    tail = jnp.where(lane >= half, packed[half : half + 1, :], 0.0)
+    out[...] = lower + jnp.where(sub == lane, tail, lower.T)
+    out[:half, :] = jnp.where((sub == lane)[:half], lower[:half], out[:half, :])
+
+
+def unpack_call(packed):
+    size = packed.shape[1]
+    return pl.pallas_call(
+        unpack_kernel,
+        out_shape=jax.ShapeDtypeStruct((size, size), jnp.float32),
+        in_specs=vmem(1),
+        out_specs=vmem(1)[0],
+        compiler_params=pltpu.CompilerParams(vmem_limit_bytes=GRANT),
+        name="unpack",
+    )(packed)
 
 
 def schur_kernel(groups, width, offsets, pieces, total, arrived, gathered, send1, recv1, send2, recv2):
@@ -213,67 +373,36 @@
 
 
 def schur_call(pieces, groups, width, offsets):
-    _, size, _ = pieces.shape
+    _, height, size = pieces.shape
     partners = len(offsets) - 1
     return pl.pallas_call(
         functools.partial(schur_kernel, groups, width, offsets),
-        out_shape=jax.ShapeDtypeStruct((size, size), jnp.float32),
-        in_specs=[pl.BlockSpec(memory_space=pltpu.VMEM)],
-        out_specs=pl.BlockSpec(memory_space=pltpu.VMEM),
+        out_shape=jax.ShapeDtypeStruct((height, size), jnp.float32),
+        in_specs=vmem(1),
+        out_specs=vmem(1)[0],
         scratch_shapes=[
-            pltpu.VMEM((partners, size, size), jnp.float32),
-            pltpu.VMEM((groups, size, size), jnp.float32),
+            pltpu.VMEM((partners, height, size), jnp.float32),
+            pltpu.VMEM((groups, height, size), jnp.float32),
             pltpu.SemaphoreType.DMA((partners,)),
             pltpu.SemaphoreType.DMA((partners,)),
             pltpu.SemaphoreType.DMA((groups - 1,)),
             pltpu.SemaphoreType.DMA((groups - 1,)),
         ],
-        compiler_params=pltpu.CompilerParams(collective_id=1, has_side_effects=True),
+        compiler_params=pltpu.CompilerParams(collective_id=1, has_side_effects=True, vmem_limit_bytes=GRANT),
+        name="sums",
     )(pieces)
 
 
-def position_codes(positions, rows, columns):
-    ratio = columns // rows
-    row_count = 5 * ratio
-    starts = [0]
-    for r in range(row_count):
-        starts.append(starts[-1] + r // ratio + 1)
-    row = sum((positions >= starts[r]).astype(jnp.int32) for r in range(1, row_count))
-    begin = sum(jnp.where(positions >= starts[r], starts[r] - starts[r - 1], 0) for r in range(1, row_count))
-    return row * 8 + positions - begin, row_count * 8
-
-
 def body(groups, width, tiles, tile_front, tile_pos, front_slot, front_parent, pivot):
-    myself = lax.axis_index("sep")
     held = tiles.shape[1]
-    rows = tiles.shape[2]
-    columns = tiles.shape[3]
-    fronts = front_slot.shape[1]
     room = max(2, -(-2 * held // width))
     offsets = (0, 1, width - 1, width // 2)
     slots = front_slot[0]
-    parents = front_parent[0]
-    front_ids = jnp.arange(fronts, dtype=jnp.int32)
-    owner_of = jnp.sum(jnp.where(tile_front[0] == front_ids[None, :], slots[None, :], 0), 1)
-    target = (owner_of[:, None] == jnp.arange(width, dtype=jnp.int32)[None, :]).astype(jnp.int32)
-    rank = jnp.sum(target * (jnp.cumsum(target, 0) - 1), 1)
-    place = owner_of * room + rank
-    codes, empty = position_codes(tile_pos[0], rows, columns)
-    outgoing = jnp.zeros((width * room, rows, columns), jnp.bfloat16).at[place].set(tiles[0])
-    labels = jnp.full((width * room,), empty, jnp.int32).at[place].set(codes)
-    arrived, labels = (
-        lax.all_to_all(outgoing.reshape(width, room, rows, columns), "sep", split_axis=0, concat_axis=0, tiled=True),
-        lax.all_to_all(labels.reshape(width, room), "sep", split_axis=0, concat_axis=0, tiled=True),
-    )
-    arrived = arrived.reshape(width * room, rows, columns)
-    labels = labels.reshape(width * room)
-    mine = slots == myself
-    pivots = jnp.sum(jnp.where(mine[:, None], pivot[0], 0.0), 0).reshape(-1, columns)
-    parent = jnp.sum(jnp.where(mine, parents, 0))
-    distance = jnp.reshape((parent - myself) % width, (1,))
-    factor, pieces = front_call(labels, distance, arrived, pivots, rows, columns, offsets)
-    total = schur_call(pieces, groups, width, offsets)
-    return (factor[None, None], total[None])
+    outgoing, labels = pack_call(tile_front.reshape(held), tile_pos[0], slots, tiles[0], width, room)
+    arrived, codes = exchange_call(outgoing, labels)
+    factor, pieces = front_call(slots, front_parent[0], codes, arrived, pivot[0], offsets, room)
+    packed = schur_call(pieces, groups, width, offsets)
+    return (factor[None, None], unpack_call(packed)[None])
 
 
 def solution(mesh):

time: 77.2 us -> 58.1 us (0.75)
  Pallas kernels: 39.7 us -> 54.2 us
  waiting for transfers between devices: 11.5 us -> 0 us
  starting transfers between devices: 9.54 us -> 0 us
  local copies, waits for them, and re-layouts: 10.6 us -> 3.01 us
  other arithmetic: 3.9 us -> 0 us
    pallas_call x1 -> x4, Pallas kernels: 25.4 us -> 43.8 us  [the longest x1 25.1 us: front_call(): pl.pallas_call(functools.partial(front_kernel, offsets, room), out_shape=...]
    all_to_all x2 -> x0, waiting for transfers between devices: 11.5 us -> none  [the longest x1 11.5 us: body(): lax.all_to_all(outgoing.reshape(width, room, rows, columns), 'sep', split...]
    all_to_all x2 -> x0, starting transfers between devices: 9.54 us -> none  [the longest x1 5.2 us: body(): lax.all_to_all(labels.reshape(width, room), 'sep', split_axis=0, concat_a...]
    scatter x2 -> x0, local copies, waits for them, and re-layouts: 5.03 us -> none  [the longest x1 4.35 us: body(): jnp.zeros((width * room, rows, columns), jnp.bfloat16).at[place]]
    pallas_call x1, Pallas kernels: 14.3 us -> 10.4 us  [schur_call(): pl.pallas_call(functools.partial(schur_kernel, groups, width, offsets), o...]
    reduce_sum x4 -> x0, other arithmetic: 2.34 us -> none  [the longest x1 0.85 us: body(): jnp.sum(jnp.where(tile_front[0] == front_ids[None, :], slots[None, :], 0)...]
    all_to_all x2 -> x0, local copies, waits for them, and re-layouts: 1.26 us -> none  [body(): lax.all_to_all(labels.reshape(width, room), 'sep', split_axis=0, concat_a...]
    broadcast_in_dim x1 -> x0, local copies, waits for them, and re-layouts: 1.22 us -> none  [body(): jnp.zeros((width * room, rows, columns), jnp.bfloat16).at[place]]
  transfers between devices with their start and end apart: 2 -> 0, of which waited for: 1 -> 0; matrix products, arithmetic and copies ran while one was open for 11% -> 0% of each run, Pallas kernels for 0% -> 0%
where the time goes in v2:
time: 58.1 us; the launch traced here: 57.9 us
  Pallas kernels  54.2 us (93%)
  local copies, waits for them, and re-layouts  3.01 us (5%)
  between operations  0.7 us (1%)
    pallas_call x1, Pallas kernels, front_call(): pl.pallas_call(functools.partial(front_kernel, offsets, room), out_shape=...  25.1 us
    pallas_call x1, Pallas kernels, exchange_call(): pl.pallas_call(functools.partial(exchange_kernel, width, order), out_shap...  17.1 us
    pallas_call x1, Pallas kernels, schur_call(): pl.pallas_call(functools.partial(schur_kernel, groups, width, offsets), o...  10.4 us
    unnamed x12, local copies, waits for them, and re-layouts  3.01 us

profile of v2, /device:TPU:0, one launch (start us, length us, event | category | flops | bytes accessed | tf_op | source)
XLA Modules:
  0.0 57.9 jit_solution(676444436416681651)
XLA Ops:
  0.6 0.0 copy-start.3
  0.6 0.0 copy-start
  0.7 1.0 %copy-done = bf16[1,32,64,128]{3,2,1,0:T(8,128)(2,1)S(1)} copy-done((bf16[1,32,64,128]{3,2,1,0:T(8,128)(2,1)S(1)}, bf16[1,32,64,128]{3,2,1,0:T(8,128)(2,1)}, u32[]{:S(2)}) %copy-start) | copy-done | bytes 524312
  1.7 0.0 copy-start.2
  1.7 0.7 %copy-done.2 = s32[1,8]{1,0:T(1,128)S(1)} copy-done((s32[1,8]{1,0:T(1,128)S(1)}, s32[1,8]{1,0:T(1,128)}, u32[]{:S(2)}) %copy-start.2) | copy-done | bytes 56
  2.3 0.0 copy-start.4
  2.3 0.7 %copy-done.4 = s32[1,32,1]{1,2,0:T(1,128)S(1)} copy-done((s32[1,32,1]{1,2,0:T(1,128)S(1)}, s32[1,32,1]{1,2,0:T(1,128)}, u32[]{:S(2)}) %copy-start.4) | copy-done | bytes 152
  3.0 0.0 copy-start.5
  3.0 0.7 %copy-done.5 = s32[1,32]{1,0:T(1,128)S(1)} copy-done((s32[1,32]{1,0:T(1,128)S(1)}, s32[1,32]{1,0:T(1,128)}, u32[]{:S(2)}) %copy-start.5) | copy-done | bytes 152
  3.7 0.0 copy-start.1
  3.7 0.8 %pack.1 = (bf16[8,8,64,128]{3,2,1,0:T(8,128)(2,1)S(1)}, s32[8,1,128]{2,1,0:T(1,128)S(1)}) custom-call(s32[32]{0:T(128)S(1)} %bitcast.13, s32[32]{0:T(128)S(1)} %bitcast.14, s32[8]{0:T(128)S(1)} %bitcast.10, bf16[32,64,128]{2,1,0:T(8,128)(2,1)S(1)} %bitcast.8), custom_call_target="tpu_custom_call" | custom-call | tf_op jit(solution)/shard_map/pack/pallas_call | solution.py:229
  4.5 17.1 %exchange.1 = (bf16[8,8,64,128]{3,2,1,0:T(8,128)(2,1)S(1)}, s32[8,1,128]{2,1,0:T(1,128)S(1)}) custom-call(bf16[8,8,64,128]{3,2,1,0:T(8,128)(2,1)S(1)} %get-tuple-element.8.outgoing, s32[8,1,128]{2,1,0:T(1,128)S(1)} %get-tuple-element.9.labels), custom_call_target="tpu_custom_call" | custom-call | tf_op jit(solution)/shard_map/exchange/pallas_call | solution.py:282
  21.6 0.0 copy-done.3
  21.6 0.0 copy-done.1
  21.6 25.1 %front.1 = (f32[640,512]{1,0:T(8,128)}, f32[4,72,128]{2,1,0:T(8,128)S(1)}) custom-call(s32[8]{0:T(128)S(1)} %bitcast.11, s32[8]{0:T(128)S(1)} %bitcast.12, s32[8,1,128]{2,1,0:T(1,128)S(1)} %get-tuple-element.10.labels, bf16[8,8,64,128]{3,2,1,0:T(8,128)(2,1)S(1)} %get-tuple-element.11.tiles, f32[8,640]{1,0:T(8,128)S(1)} %bitcast.9), custom_call_target="tpu_custom_call" | custom-call | tf_op jit(solution)/shard_map/front/pallas_call | solution.py:174
  46.7 10.4 %sums.1.packed = f32[72,128]{1,0:T(8,128)S(1)} custom-call(f32[4,72,128]{2,1,0:T(8,128)S(1)} %get-tuple-element.13.pieces), custom_call_target="tpu_custom_call" | custom-call | tf_op jit(solution)/shard_map/sums/pallas_call | solution.py:378
  57.1 0.8 %unpack.1 = f32[128,128]{1,0:T(8,128)} custom-call(f32[72,128]{1,0:T(8,128)S(1)} %sums.1.packed), custom_call_target="tpu_custom_call" | custom-call | tf_op jit(solution)/shard_map/unpack/pallas_call | solution.py:314
Async XLA Ops:
  0.6 20.9 %copy-start.3 = (s32[1,8]{1,0:T(1,128)S(1)}, s32[1,8]{1,0:T(1,128)}, u32[]{:S(2)}) copy-start(s32[1,8]{1,0:T(1,128)} %param.10) | copy-start | bytes 100
  0.6 1.0 %copy-start = (bf16[1,32,64,128]{3,2,1,0:T(8,128)(2,1)S(1)}, bf16[1,32,64,128]{3,2,1,0:T(8,128)(2,1)}, u32[]{:S(2)}) copy-start(bf16[1,32,64,128]{3,2,1,0:T(8,128)(2,1)} %param.6) | copy-start | bytes 1572868
  1.7 0.7 %copy-start.2 = (s32[1,8]{1,0:T(1,128)S(1)}, s32[1,8]{1,0:T(1,128)}, u32[]{:S(2)}) copy-start(s32[1,8]{1,0:T(1,128)} %param.9) | copy-start | bytes 100
  2.3 0.7 %copy-start.4 = (s32[1,32,1]{1,2,0:T(1,128)S(1)}, s32[1,32,1]{1,2,0:T(1,128)}, u32[]{:S(2)}) copy-start(s32[1,32,1]{1,2,0:T(1,128)} %param.7) | copy-start | bytes 388
  3.0 0.7 %copy-start.5 = (s32[1,32]{1,0:T(1,128)S(1)}, s32[1,32]{1,0:T(1,128)}, u32[]{:S(2)}) copy-start(s32[1,32]{1,0:T(1,128)} %param.8) | copy-start | bytes 388
  3.7 17.9 %copy-start.1 = (f32[1,8,640]{2,1,0:T(8,128)S(1)}, f32[1,8,640]{2,1,0:T(8,128)}, u32[]{:S(2)}) copy-start(f32[1,8,640]{2,1,0:T(8,128)} %param.11) | copy-start | bytes 61444

commit v3 on v2

--- a/solution.py
+++ b/solution.py
@@ -22,6 +22,10 @@
 
 def sublanes(x, r):
     return jnp.broadcast_to(x[r : r + 1, :], x.shape)
+
+
+def corner(x, s, j):
+    return jnp.take_along_axis(lanes(x, j), jnp.full(x.shape, s, jnp.int32), axis=0)
 
 
 def factor_diagonal(a_ref, u_ref, w_ref):
@@ -33,40 +37,50 @@
     w = [jnp.where(lane == sub + PANEL * i, 1.0, 0.0) for i in range(panels)]
     for p in range(panels):
         j0 = PANEL * p
-        cols = [lanes(a[p], j0 + r) for r in range(PANEL)]
-        b = [[sublanes(cols[r], s) for s in range(r + 1)] for r in range(PANEL)]
         ta = [sublanes(a[p], r) for r in range(PANEL)]
+        b = [[corner(a[p], s, j0 + r) for s in range(r + 1)] for r in range(PANEL)]
         tw = [sublanes(w[p], r) for r in range(PANEL)]
-        inv = [None] * PANEL
-        n = [[None] * PANEL for _ in range(PANEL)]
-        for r in range(PANEL):
-            inv[r] = 1.0 / b[r][r]
-            for s in range(r + 1, PANEL):
-                n[s][r] = b[s][r] * inv[r]
-            for s in range(r + 1, PANEL):
-                for t in range(r + 1, s + 1):
-                    b[s][t] = b[s][t] - n[s][r] * b[t][r]
-            for s in range(r + 1, PANEL):
-                ta[s] = ta[s] - n[s][r] * ta[r]
-                tw[s] = tw[s] - n[s][r] * tw[r]
-        u = ta[0] * lax.rsqrt(b[0][0])
-        v = tw[0] * lax.rsqrt(b[0][0])
-        for r in range(1, PANEL):
-            root = lax.rsqrt(b[r][r])
-            u = jnp.where(sub == r, ta[r] * root, u)
-            v = jnp.where(sub == r, tw[r] * root, v)
+        idet = [None] * PANEL
+        m = [[None] * PANEL for _ in range(PANEL)]
+        for r in range(0, PANEL, 2):
+            q = r + 1
+            idet[r] = 1.0 / (b[r][r] * b[q][q] - b[q][r] * b[q][r])
+            for s in range(r + 2, PANEL):
+                m[s][r] = (b[s][r] * b[q][q] - b[s][q] * b[q][r]) * idet[r]
+                m[s][q] = (b[s][q] * b[r][r] - b[s][r] * b[q][r]) * idet[r]
+            for s in range(r + 2, PANEL):
+                for t in range(r + 2, s + 1):
+                    b[s][t] = b[s][t] - (m[s][r] * b[t][r] + m[s][q] * b[t][q])
+            for s in range(r + 2, PANEL):
+                ta[s] = ta[s] - (m[s][r] * ta[r] + m[s][q] * ta[q])
+                tw[s] = tw[s] - (m[s][r] * tw[r] + m[s][q] * tw[q])
+        u = v = None
+        for r in range(0, PANEL, 2):
+            q = r + 1
+            lead = lax.rsqrt(b[r][r])
+            ratio = b[q][r] / b[r][r]
+            root = lax.rsqrt(b[q][q] - ratio * b[q][r])
+            ua, va = ta[r] * lead, tw[r] * lead
+            ub, vb = (ta[q] - ratio * ta[r]) * root, (tw[q] - ratio * tw[r]) * root
+            u = ua if r == 0 else jnp.where(sub == r, ua, u)
+            v = va if r == 0 else jnp.where(sub == r, va, v)
+            u = jnp.where(sub == q, ub, u)
+            v = jnp.where(sub == q, vb, v)
         u_ref[j0 : j0 + PANEL, :] = jnp.where(lane >= sub + j0, u, 0.0)
         w_ref[j0 : j0 + PANEL, :] = v
         if p + 1 < panels:
             ya = [None] * PANEL
             yw = [None] * PANEL
-            for r in reversed(range(PANEL)):
-                ya[r] = ta[r] * inv[r]
-                yw[r] = tw[r] * inv[r]
-            for r in reversed(range(PANEL)):
+            for r in range(0, PANEL, 2):
+                q = r + 1
+                x, y, z = b[r][r] * idet[r], b[q][r] * idet[r], b[q][q] * idet[r]
+                for got, t in ((ya, ta), (yw, tw)):
+                    got[r] = z * t[r] - y * t[q]
+                    got[q] = x * t[q] - y * t[r]
+            for r in reversed(range(0, PANEL, 2)):
                 for s in range(r):
-                    ya[s] = ya[s] - n[r][s] * ya[r]
-                    yw[s] = yw[s] - n[r][s] * yw[r]
+                    ya[s] = ya[s] - (m[r][s] * ya[r] + m[r + 1][s] * ya[r + 1])
+                    yw[s] = yw[s] - (m[r][s] * yw[r] + m[r + 1][s] * yw[r + 1])
             for i in range(p + 1, panels):
                 for s in range(PANEL):
                     c = lanes(a[i], j0 + s)
@@ -204,20 +218,26 @@
     return jnp.where(positions < 0, row_count * 8, row * 8 + positions - begin)
 
 
-def pack_kernel(fronts, positions, slots, tiles, outgoing, labels, counts):
+def pack_kernel(fronts_in, positions_in, slots_in, tiles_in, outgoing, labels, fronts, positions, slots, tiles, counts, sem):
+    pairs = ((tiles_in, tiles), (fronts_in, fronts), (positions_in, positions), (slots_in, slots))
+    copies = [pltpu.make_async_copy(src, dst, sem.at[n]) for n, (src, dst) in enumerate(pairs)]
+    for copy in copies:
+        copy.start()
     width = outgoing.shape[0]
     held, rows, columns = tiles.shape
     labels[...] = jnp.full(labels.shape, -1, jnp.int32)
     lane = lax.broadcasted_iota(jnp.int32, labels.shape[1:], 1)
     for d in range(width):
         counts[d] = 0
+    for copy in copies:
+        copy.wait()
 
     def place(i, carry):
-        owner = slots[fronts[i]]
+        owner = slots[0, fronts[0, i]]
         rank = counts[owner]
         counts[owner] = rank + 1
         outgoing[owner, rank] = tiles[i]
-        labels[owner] = jnp.where(lane == rank, positions[i], labels[owner])
+        labels[owner] = jnp.where(lane == rank, positions[0, i], labels[owner])
         return carry
 
     lax.fori_loop(0, held, place, 0, unroll=4)
@@ -232,12 +252,19 @@
             jax.ShapeDtypeStruct((width, room, rows, columns), tiles.dtype),
             jax.ShapeDtypeStruct((width, 1, 128), jnp.int32),
         ),
-        in_specs=smem(3) + vmem(1),
+        in_specs=[pl.BlockSpec(memory_space=pltpu.HBM)] * 4,
         out_specs=vmem(2),
-        scratch_shapes=[pltpu.SMEM((width,), jnp.int32)],
+        scratch_shapes=[
+            pltpu.SMEM(fronts.shape, jnp.int32),
+            pltpu.SMEM(positions.shape, jnp.int32),
+            pltpu.SMEM(slots.shape, jnp.int32),
+            pltpu.VMEM(tiles.shape, tiles.dtype),
+            pltpu.SMEM((width,), jnp.int32),
+            pltpu.SemaphoreType.DMA((4,)),
+        ],
         compiler_params=pltpu.CompilerParams(vmem_limit_bytes=GRANT),
         name="pack",
-    )(fronts, positions, slots, tiles)
+    )(*(pltpu.with_memory_space_constraint(x, pltpu.HBM) for x in (fronts, positions, slots, tiles)))
 
 
 def exchange_kernel(width, order, outgoing, labels, arrived, codes, send, recv, lsend, lrecv, own):
@@ -398,7 +425,7 @@
     room = max(2, -(-2 * held // width))
     offsets = (0, 1, width - 1, width // 2)
     slots = front_slot[0]
-    outgoing, labels = pack_call(tile_front.reshape(held), tile_pos[0], slots, tiles[0], width, room)
+    outgoing, labels = pack_call(tile_front.reshape(1, held), tile_pos, front_slot, tiles[0], width, room)
     arrived, codes = exchange_call(outgoing, labels)
     factor, pieces = front_call(slots, front_parent[0], codes, arrived, pivot[0], offsets, room)
     packed = schur_call(pieces, groups, width, offsets)

time: 58.1 us -> 50.6 us (0.87)
  Pallas kernels: 54.2 us -> 49.9 us
  local copies, waits for them, and re-layouts: 3.01 us -> 0.01 us
    pallas_call x1, Pallas kernels: 25.1 us -> 19.9 us  [front_call(): pl.pallas_call(functools.partial(front_kernel, offsets, room), out_shape=...]
    unnamed x12 -> x6, local copies, waits for them, and re-layouts: 3.01 us -> 0.01 us
where the time goes in v3:
time: 50.6 us
  Pallas kernels  49.9 us (99%)
  between operations  0.71 us (1%)
    pallas_call x1, Pallas kernels, front_call(): pl.pallas_call(functools.partial(front_kernel, offsets, room), out_shape=...  19.9 us
    pallas_call x1, Pallas kernels, exchange_call(): pl.pallas_call(functools.partial(exchange_kernel, width, order), out_shap...  17.1 us
    pallas_call x1, Pallas kernels, schur_call(): pl.pallas_call(functools.partial(schur_kernel, groups, width, offsets), o...  10.8 us
    pallas_call x1, Pallas kernels, pack_call(): pl.pallas_call(pack_kernel, out_shape=(jax.ShapeDtypeStruct((width, room,...  1.39 us

profile of v3, /device:TPU:0, one launch (start us, length us, event | category | flops | bytes accessed | tf_op | source)
XLA Modules:
  0.0 50.6 jit_solution(13149457437310513805)
XLA Ops:
  0.6 0.0 copy-start.1
  0.6 0.0 copy-start
  0.7 0.0 copy-start.2
  0.7 1.4 %pack.1 = (bf16[8,8,64,128]{3,2,1,0:T(8,128)(2,1)S(1)}, s32[8,1,128]{2,1,0:T(1,128)S(1)}) custom-call(s32[1,32]{1,0:T(1,128)} %bitcast.12, s32[1,32]{1,0:T(1,128)} %positions_in.1, s32[1,8]{1,0:T(1,128)} %slots_in.1, bf16[32,64,128]{2,1,0:T(8,128)(2,1)} %bitcast.10), custom_call_target="tpu_custom_call" | custom-call | tf_op jit(solution)/shard_map/pack/pallas_call | solution.py:249
  2.1 17.1 %exchange.1 = (bf16[8,8,64,128]{3,2,1,0:T(8,128)(2,1)S(1)}, s32[8,1,128]{2,1,0:T(1,128)S(1)}) custom-call(bf16[8,8,64,128]{3,2,1,0:T(8,128)(2,1)S(1)} %get-tuple-element.8.outgoing, s32[8,1,128]{2,1,0:T(1,128)S(1)} %get-tuple-element.9.labels), custom_call_target="tpu_custom_call" | custom-call | tf_op jit(solution)/shard_map/exchange/pallas_call | solution.py:309
  19.1 0.0 copy-done.1
  19.1 0.0 copy-done
  19.1 0.0 copy-done.2
  19.2 19.9 %front.1 = (f32[640,512]{1,0:T(8,128)}, f32[4,72,128]{2,1,0:T(8,128)S(1)}) custom-call(s32[8]{0:T(128)S(1)} %bitcast.8, s32[8]{0:T(128)S(1)} %bitcast.9, s32[8,1,128]{2,1,0:T(1,128)S(1)} %get-tuple-element.10.labels, bf16[8,8,64,128]{3,2,1,0:T(8,128)(2,1)S(1)} %get-tuple-element.11.tiles, f32[8,640]{1,0:T(8,128)S(1)} %bitcast.7), custom_call_target="tpu_custom_call" | custom-call | tf_op jit(solution)/shard_map/front/pallas_call | solution.py:188
  39.0 10.8 %sums.1.packed = f32[72,128]{1,0:T(8,128)S(1)} custom-call(f32[4,72,128]{2,1,0:T(8,128)S(1)} %get-tuple-element.13.pieces), custom_call_target="tpu_custom_call" | custom-call | tf_op jit(solution)/shard_map/sums/pallas_call | solution.py:405
  49.8 0.8 %unpack.1 = f32[128,128]{1,0:T(8,128)} custom-call(f32[72,128]{1,0:T(8,128)S(1)} %sums.1.packed), custom_call_target="tpu_custom_call" | custom-call | tf_op jit(solution)/shard_map/unpack/pallas_call | solution.py:341
Async XLA Ops:
  0.6 18.5 %copy-start.1 = (s32[1,8]{1,0:T(1,128)S(1)}, s32[1,8]{1,0:T(1,128)}, u32[]{:S(2)}) copy-start(s32[1,8]{1,0:T(1,128)} %slots_in.1) | copy-start | bytes 100
  0.6 18.5 %copy-start = (f32[1,8,640]{2,1,0:T(8,128)S(1)}, f32[1,8,640]{2,1,0:T(8,128)}, u32[]{:S(2)}) copy-start(f32[1,8,640]{2,1,0:T(8,128)} %param.11) | copy-start | bytes 61444
  0.7 18.5 %copy-start.2 = (s32[1,8]{1,0:T(1,128)S(1)}, s32[1,8]{1,0:T(1,128)}, u32[]{:S(2)}) copy-start(s32[1,8]{1,0:T(1,128)} %param.10) | copy-start | bytes 100

commit v4 on v3

--- a/solution.py
+++ b/solution.py
@@ -90,7 +90,7 @@
                 w[i] = w[i] - w_new
 
 
-def front_kernel(offsets, room, slots, parents, labels, tiles, pivots, factor_ref, pieces_ref, codes, acc, diag, up, winv, schur_ref, sem):
+def front_kernel(offsets, room, slots, parents, labels, tiles, pivots, factor_out, pieces_ref, codes, acc, diag, up, winv, schur_ref, sem, factor_ref, written):
     width, _, rows, size = tiles.shape
     blocks = acc.shape[0]
     elim = blocks - 1
@@ -137,6 +137,9 @@
             acc[j, span(i), :] = -half
         acc[j, span(j), :] = jnp.where(sub == lane, sums + row_sums[j], -mixed)
 
+    def write(j):
+        return pltpu.make_async_copy(factor_ref.at[:, span(j)], factor_out.at[:, span(j)], written.at[j])
+
     def step(k, carry):
         diag[...] = acc[k, pl.ds(pl.multiple_of(k * size, size), size), :]
         factor_diagonal(diag, up, winv)
@@ -152,6 +155,7 @@
                 for j in range(kk + 1, elim):
                     o = (j - kk - 1) * size
                     acc[j, j * size : blocks * size, :] -= dot_nt(below[o:, :], below[o : o + size, :])
+                write(kk).start()
                 last = below[(elim - kk - 1) * size :, :]
                 if kk == 0:
                     schur_ref[...] = dot_nt(last, last)
@@ -171,6 +175,8 @@
     for n, offset in enumerate(offsets):
         pieces_ref[n, :half, :] = jnp.where(distance == offset, packed, 0.0)
         pieces_ref[n, half:, :] = jnp.where(distance == offset, tail, 0.0)
+    for j in range(elim):
+        write(j).wait()
 
 
 def vmem(count):
@@ -192,7 +198,7 @@
             jax.ShapeDtypeStruct((len(offsets), columns // 2 + 8, columns), jnp.float32),
         ),
         in_specs=smem(2) + vmem(3),
-        out_specs=vmem(2),
+        out_specs=[pl.BlockSpec(memory_space=pltpu.HBM)] + vmem(1),
         scratch_shapes=[
             pltpu.SMEM(labels.shape, jnp.int32),
             pltpu.VMEM((order // columns, order + rows, columns), jnp.float32),
@@ -201,6 +207,8 @@
             square,
             square,
             pltpu.SemaphoreType.DMA,
+            pltpu.VMEM((order, order - columns), jnp.float32),
+            pltpu.SemaphoreType.DMA((order // columns - 1,)),
         ],
         compiler_params=pltpu.CompilerParams(vmem_limit_bytes=GRANT),
         name="front",

time: 50.6 us -> 50.1 us (level)
  Pallas kernels: 49.9 us -> 49.2 us
where the time goes in v4:
time: 50.1 us; the launch traced here: 49.9 us
  Pallas kernels  49.2 us (98%)
  between operations  0.71 us (1%)
    pallas_call x1, Pallas kernels, front_call(): pl.pallas_call(functools.partial(front_kernel, offsets, room), out_shape=...  19.5 us
    pallas_call x1, Pallas kernels, exchange_call(): pl.pallas_call(functools.partial(exchange_kernel, width, order), out_shap...  17.1 us
    pallas_call x1, Pallas kernels, schur_call(): pl.pallas_call(functools.partial(schur_kernel, groups, width, offsets), o...  10.5 us
    pallas_call x1, Pallas kernels, pack_call(): pl.pallas_call(pack_kernel, out_shape=(jax.ShapeDtypeStruct((width, room,...  1.39 us

profile of v4, /device:TPU:0, one launch (start us, length us, event | category | flops | bytes accessed | tf_op | source)
XLA Modules:
  0.0 49.9 jit_solution(13438920564147648809)
XLA Ops:
  0.6 0.0 copy-start.1
  0.6 0.0 copy-start
  0.7 0.0 copy-start.2
  0.7 1.4 %pack.1 = (bf16[8,8,64,128]{3,2,1,0:T(8,128)(2,1)S(1)}, s32[8,1,128]{2,1,0:T(1,128)S(1)}) custom-call(s32[1,32]{1,0:T(1,128)} %bitcast.12, s32[1,32]{1,0:T(1,128)} %positions_in.1, s32[1,8]{1,0:T(1,128)} %slots_in.1, bf16[32,64,128]{2,1,0:T(8,128)(2,1)} %bitcast.10), custom_call_target="tpu_custom_call" | custom-call | tf_op jit(solution)/shard_map/pack/pallas_call | solution.py:257
  2.1 17.1 %exchange.1 = (bf16[8,8,64,128]{3,2,1,0:T(8,128)(2,1)S(1)}, s32[8,1,128]{2,1,0:T(1,128)S(1)}) custom-call(bf16[8,8,64,128]{3,2,1,0:T(8,128)(2,1)S(1)} %get-tuple-element.8.outgoing, s32[8,1,128]{2,1,0:T(1,128)S(1)} %get-tuple-element.9.labels), custom_call_target="tpu_custom_call" | custom-call | tf_op jit(solution)/shard_map/exchange/pallas_call | solution.py:317
  19.1 0.0 copy-done.1
  19.1 0.0 copy-done
  19.1 0.0 copy-done.2
  19.2 19.5 %front.1 = (f32[640,512]{1,0:T(8,128)}, f32[4,72,128]{2,1,0:T(8,128)S(1)}) custom-call(s32[8]{0:T(128)S(1)} %bitcast.8, s32[8]{0:T(128)S(1)} %bitcast.9, s32[8,1,128]{2,1,0:T(1,128)S(1)} %get-tuple-element.10.labels, bf16[8,8,64,128]{3,2,1,0:T(8,128)(2,1)S(1)} %get-tuple-element.11.tiles, f32[8,640]{1,0:T(8,128)S(1)} %bitcast.7), custom_call_target="tpu_custom_call" | custom-call | tf_op jit(solution)/shard_map/front/pallas_call | solution.py:194
  38.6 10.5 %sums.1.packed = f32[72,128]{1,0:T(8,128)S(1)} custom-call(f32[4,72,128]{2,1,0:T(8,128)S(1)} %get-tuple-element.13.pieces), custom_call_target="tpu_custom_call" | custom-call | tf_op jit(solution)/shard_map/sums/pallas_call | solution.py:413
  49.1 0.8 %unpack.1 = f32[128,128]{1,0:T(8,128)} custom-call(f32[72,128]{1,0:T(8,128)S(1)} %sums.1.packed), custom_call_target="tpu_custom_call" | custom-call | tf_op jit(solution)/shard_map/unpack/pallas_call | solution.py:349
Async XLA Ops:
  0.6 18.5 %copy-start.1 = (s32[1,8]{1,0:T(1,128)S(1)}, s32[1,8]{1,0:T(1,128)}, u32[]{:S(2)}) copy-start(s32[1,8]{1,0:T(1,128)} %slots_in.1) | copy-start | bytes 100
  0.6 18.5 %copy-start = (f32[1,8,640]{2,1,0:T(8,128)S(1)}, f32[1,8,640]{2,1,0:T(8,128)}, u32[]{:S(2)}) copy-start(f32[1,8,640]{2,1,0:T(8,128)} %param.11) | copy-start | bytes 61444
  0.7 18.5 %copy-start.2 = (s32[1,8]{1,0:T(1,128)S(1)}, s32[1,8]{1,0:T(1,128)}, u32[]{:S(2)}) copy-start(s32[1,8]{1,0:T(1,128)} %param.10) | copy-start | bytes 100
